TPU v7x, 32 devices: a whole 2x2x4 slice. The times are simulated.
32 devices in a mesh: frame: 2 (over y), plane: 16 (over z, x, core).
Axes of the slice: x: 2, y: 2, z: 4, core: 2. Of those that a mesh axis runs over, the one named last changes fastest.
Arguments:
- states: float32 [4, 2, 16, 256, 256], P(None, 'frame', 'plane'), may hold values from -6 to 6
- measured: float32 [2, 16, 256, 256], P('frame', 'plane'), may hold values from -6 to 6
- response: float32 [256, 256], replicated, may hold values from 0.1 to 10
- kernel_in: bfloat16 [3, 9, 32, 2], replicated, may hold values from -1.5 to 1.5
- bias_in: float32 [3, 32], replicated, may hold values from -3 to 3
- kernel_mid: bfloat16 [3, 1, 9, 32, 32], replicated, may hold values from -0.375 to 0.375
- bias_mid: float32 [3, 1, 32], replicated, may hold values from -3 to 3
- kernel_out: bfloat16 [3, 9, 32], replicated, may hold values from -0.375 to 0.375
Outputs:
- new_states: float32 [4, 2, 16, 256, 256], P(None, 'frame', 'plane')
All inputs are finite; a program needn't handle non-finite values.
Results may differ from a plain program's by a relative error of at most 0.0056.
Values may be sent and summed in bfloat16 or wider, within the bound.
No kernel may reach another device: no remote copies, remote signals or barrier semaphores. Data moves between devices by JAX's collectives and lax.ppermute only.
A program may use at most 192 MiB of HBM per device.

v0:
```python
import functools
import math

import jax
import jax.numpy as jnp
import numpy as np
from jax import lax
from jax.experimental import pallas as pl
from jax.experimental.pallas import tpu as pltpu
from jax.sharding import PartitionSpec as P

relaxation = 0.8

BF = jnp.bfloat16
F32 = jnp.float32

CHUNK = 16
WINDOW = 32
LEAD = 8

FIRST_TAP = {(0, 3): 0, (0, 0): 1, (0, 1): 2, (1, 0): 0, (1, 1): 1, (1, 2): 2}
LATER_TAP = {
    (0, 0, 0): 1, (0, 0, 1): 2, (1, 0, 1): 0,
    (0, 1, 0): 0, (0, 1, 1): 1, (1, 1, 0): 2,
}


def fourier_tables(length):
    indices = np.arange(length, dtype=np.int64)
    phase = indices[:, None] * indices[None, :] % length
    angle = phase.astype(np.float32) * np.float32(2.0 * math.pi / length)
    return np.cos(angle).astype(BF), np.sin(angle).astype(BF)


def mm(a, b):
    return jnp.dot(a, b, preferred_element_type=F32)


def nt(a, b):
    return lax.dot_general(a, b, (((1,), (1,)), ((), ())), preferred_element_type=F32)


def tn(a, b):
    return lax.dot_general(a, b, (((0,), (0,)), ((), ())), preferred_element_type=F32)


def iota(shape, axis):
    return lax.broadcasted_iota(jnp.int32, shape, axis)


def parity_matrix(n):
    half = n // 2
    row, col = iota((n, n), 0), iota((n, n), 1)
    natural = jnp.where(col < half, 2 * col, 2 * (col - half) + 1)
    return (row == natural).astype(F32).astype(BF)


def whole(shape):
    zeros = (0,) * len(shape)
    return pl.BlockSpec(shape, lambda i: zeros)


def agent(k, n):
    return pl.BlockSpec((1, n, n), lambda i: (k, 0, 0))


def cost(flops, moved):
    return pl.CostEstimate(flops=flops, bytes_accessed=moved, transcendentals=0)


def spread_kernel(devices, fast, w1, w2, w3, z_ref, *outs):
    n = w1.shape[1]
    split = parity_matrix(n)
    z_ref[...] = mm(w1[0].astype(BF), split).astype(BF)
    toward_x = tn(w2[0].astype(BF), split)
    toward_y = mm(w3[0].astype(BF), split)
    if fast:
        per = n // devices
        both = jnp.concatenate(
            [toward_x.reshape(devices, per, n), toward_y.reshape(devices, per, n)], 1
        )
        outs[0][...] = both.reshape(2 * n, n).astype(BF)
    else:
        outs[0][...] = toward_x.astype(BF)
        outs[1][...] = toward_y.astype(BF)


def spread(current, devices):
    n = current.shape[1]
    per = n // devices
    fast = per % 8 == 0
    plane = jax.ShapeDtypeStruct((n, n), BF)
    shapes = [plane, jax.ShapeDtypeStruct((2 * n, n), BF)] if fast else [plane] * 3
    outs = pl.pallas_call(
        functools.partial(spread_kernel, devices, fast),
        out_shape=shapes,
        grid=(1,),
        in_specs=[agent(1, n), agent(2, n), agent(3, n)],
        out_specs=[whole(s.shape) for s in shapes],
        cost_estimate=cost(6 * n**3, 18 * n * n),
        name="spread",
    )(current, current, current)
    if fast:
        return outs[0], outs[1]
    parts = [o.reshape(devices, per, n) for o in outs[1:]]
    return outs[0], jnp.concatenate(parts, 1).reshape(2 * n, n)


def build_first(taps, channels):
    wide = 8 * WINDOW
    lane = iota((channels, wide), 1)
    at_row = lane % WINDOW
    pick_row = iota((6, wide), 0)
    pick_lane = iota((6, wide), 1) // WINDOW
    vectors = {}
    for parity in range(2):
        pick = jnp.zeros((6, wide), F32)
        for group in range(4):
            tap = FIRST_TAP.get((parity, group))
            if tap is not None:
                for source in range(2):
                    hit = (pick_row == 2 * tap + source) & (pick_lane == 4 * source + group)
                    pick = jnp.where(hit, 1.0, pick)
        pick = pick.astype(BF)
        for p in range(3):
            vectors[parity, p] = mm(taps[p], pick)
    pieces = []
    for row in range(CHUNK):
        for parity in range(2):
            piece = jnp.zeros((channels, wide), F32)
            for p in range(3):
                piece = jnp.where(at_row == row + LEAD - 1 + p, vectors[parity, p], piece)
            pieces.append(piece.astype(BF))
    return pieces


def build_mid(taps, channels):
    wide = 8 * channels
    block = iota((channels, wide), 1) // channels
    repeat = (iota((channels, wide), 0) == iota((channels, wide), 1) % channels).astype(F32).astype(BF)
    spread_taps = mm(taps, repeat)
    pieces = []
    for shifted in range(2):
        for row in range(2):
            for parity in range(2):
                piece = jnp.zeros((channels, wide), F32)
                for p in range(3):
                    for source in range(2):
                        tap = LATER_TAP.get((shifted, parity, source))
                        if tap is not None:
                            t = 3 * p + tap
                            value = spread_taps[t * channels : (t + 1) * channels]
                            piece = jnp.where(block == 2 * (row + p) + source, value, piece)
                pieces.append(piece.astype(BF))
    return pieces


def build_last(taps, channels):
    wide = (CHUNK + 2) * 2 * channels
    lane = iota((channels, wide), 1)
    at_row = iota((CHUNK, wide), 1) // (2 * channels)
    out_row = iota((CHUNK, wide), 0)
    spread_taps = []
    for source in range(2):
        hit = (lane % channels == iota((channels, wide), 0)) & (lane // channels % 2 == source)
        spread_taps.append(mm(taps, hit.astype(F32).astype(BF)))
    pieces = []
    for shifted in range(2):
        for parity in range(2):
            piece = jnp.zeros((CHUNK, wide), F32)
            for p in range(3):
                value = jnp.zeros((1, wide), F32)
                for source in range(2):
                    tap = LATER_TAP.get((shifted, parity, source))
                    if tap is not None:
                        t = 3 * p + tap
                        value = value + spread_taps[source][t : t + 1]
                piece = jnp.where(at_row == out_row + p, value, piece)
            pieces.append(piece.astype(BF))
    return pieces


def column(row_vector, lanes):
    size = row_vector.shape[1]
    square = iota((size, size), 0) == iota((size, size), 1)
    spread_rows = jnp.where(square, jnp.broadcast_to(row_vector, (size, size)), 0.0)
    return jnp.broadcast_to(jnp.sum(spread_rows, 1, keepdims=True), (size, lanes))


def prepare_kernel(
    w0, measured, response, cos_ref, sin_ref, kin, bin_, kmid, bmid, kout,
    data_ref, first_ref, mid_ref, last_ref, bias_ref,
):
    n = response.shape[0]
    channels = kmid.shape[2]
    lanes = bias_ref.shape[3]
    cosine, sines = cos_ref[...], sin_ref[...]
    gain = 1.0 / (1.0 + response[...])
    source = (measured[0] + w0[0]).astype(BF)
    row_real = mm(source, cosine).astype(BF)
    row_imag = (-mm(source, sines)).astype(BF)
    spec_real = ((mm(cosine, row_real) + mm(sines, row_imag)) * gain).astype(BF)
    spec_imag = ((mm(cosine, row_imag) - mm(sines, row_real)) * gain).astype(BF)
    back_real = (mm(cosine, spec_real) - mm(sines, spec_imag)).astype(BF)
    back_imag = (mm(cosine, spec_imag) + mm(sines, spec_real)).astype(BF)
    data_ref[...] = (mm(back_real, cosine) - mm(back_imag, sines)) * (1.0 / (n * n))
    for which in range(3):
        for index, piece in enumerate(build_first([kin[which, p] for p in range(3)], channels)):
            first_ref[which, pl.ds(index * channels, channels), :] = piece
        for index, piece in enumerate(build_mid(kmid[which], channels)):
            mid_ref[which, pl.ds(index * channels, channels), :] = piece
        for index, piece in enumerate(build_last(kout[which], channels)):
            last_ref[which, pl.ds(index * CHUNK, CHUNK), :] = piece
        bias_ref[which, 0] = column(bin_[pl.ds(which, 1), :], lanes)
        bias_ref[which, 1] = column(bmid[pl.ds(which, 1), :], lanes)


def prepare(current, measured, response, kernel_in, bias_in, kernel_mid, bias_mid, kernel_out):
    n = response.shape[0]
    channels = bias_in.shape[1]
    lanes = n // 2
    cosine, sines = fourier_tables(n)
    kin = kernel_in.reshape(3, 3, 3, channels, 2).transpose(0, 1, 3, 2, 4).reshape(3, 3, channels, 6)
    kmid = kernel_mid[:, 0].reshape(3, 9 * channels, channels)
    bmid = bias_mid[:, 0]
    wide = (CHUNK + 2) * 2 * channels
    shapes = [
        jax.ShapeDtypeStruct((n, n), F32),
        jax.ShapeDtypeStruct((3, CHUNK * 2 * channels, 8 * WINDOW), BF),
        jax.ShapeDtypeStruct((3, 8 * channels, 8 * channels), BF),
        jax.ShapeDtypeStruct((3, 4 * CHUNK, wide), BF),
        jax.ShapeDtypeStruct((3, 2, channels, lanes), F32),
    ]
    args = [response, jnp.asarray(cosine), jnp.asarray(sines), kin, bias_in, kmid, bmid, kernel_out]
    return pl.pallas_call(
        prepare_kernel,
        out_shape=shapes,
        grid=(1,),
        in_specs=[agent(0, n), agent(0, n)] + [whole(a.shape) for a in args],
        out_specs=[whole(s.shape) for s in shapes],
        cost_estimate=cost(40 * n**3, 40 * n * n),
        name="prepare",
    )(current, measured, *args)


def shifted_columns(values, parity, lanes):
    lane = iota((values.shape[0], lanes), 1)
    pieces = []
    for start in range(0, values.shape[1], lanes):
        part = values[:, start : start + lanes]
        if parity == 0:
            part = jnp.where(lane == 0, 0.0, pltpu.roll(part, 1, 1))
        else:
            part = jnp.where(lane == lanes - 1, 0.0, pltpu.roll(part, lanes - 1, 1))
        pieces.append(part)
    return jnp.concatenate(pieces, 1) if len(pieces) > 1 else pieces[0]


def halve(value):
    return jnp.maximum(value.astype(BF), jnp.zeros((), BF))


def first_layer(window, weights, bias, hidden_ref, base, channels):
    step = 8 * channels
    for index in range(CHUNK * 2 * channels // step):
        product = mm(weights[pl.ds(index * step, step), :], window)
        for part in range(step // channels):
            piece = product[part * channels : (part + 1) * channels] + bias
            hidden_ref[pl.ds(base + index * step + part * channels, channels), :] = halve(piece)


def mid_layer(slab, weights, bias, out_ref, base, channels, lanes):
    product = mm(weights, slab)
    for part in range(4):
        kept = product[part * channels : (part + 1) * channels]
        moved = product[(4 + part) * channels : (5 + part) * channels]
        piece = kept + shifted_columns(moved, part % 2, lanes) + bias
        out_ref[pl.ds(base + part * channels, channels), :] = halve(piece)


def last_layer(slab, weights, lanes):
    product = mm(weights, slab)
    return [
        product[parity * CHUNK : (parity + 1) * CHUNK]
        + shifted_columns(product[(2 + parity) * CHUNK : (3 + parity) * CHUNK], parity, lanes)
        for parity in range(2)
    ]


def planes_kernel(
    frames, depth, per, channels,
    arrived_ref, first_ref, mid_ref, last_ref, bias_ref, out_ref,
    source, result, window, hidden, deeper,
):
    lanes = arrived_ref.shape[1] // 2
    stride = 2 * per
    row = 2 * channels
    for half in range(2):
        source[half] = arrived_ref[:, half * lanes : (half + 1) * lanes].astype(F32)
    window[...] = jnp.zeros_like(window)
    for ref in (hidden, deeper):
        ref[0:row, :] = jnp.zeros((row, frames * lanes), BF)
        ref[pl.ds(row * (depth + 1), row), :] = jnp.zeros((row, frames * lanes), BF)

    def pair(step, _):
        which = step // per + 1
        for frame in range(frames):
            base = frame * depth * stride + step
            even = source[0, pl.ds(base, depth, stride), :]
            odd = source[1, pl.ds(base, depth, stride), :]
            groups = [even, odd, shifted_columns(even, 1, lanes), shifted_columns(odd, 0, lanes)]
            for image in range(frames):
                channel = (frame - image) % frames
                for group in range(4):
                    window[4 * channel + group, pl.ds(LEAD, depth), pl.ds(image * lanes, lanes)] = groups[group]
        bias1 = jnp.concatenate([bias_ref[which, 0]] * frames, 1)
        bias2 = jnp.concatenate([bias_ref[which, 1]] * frames, 1)
        for chunk in range(depth // CHUNK):
            rows = window[:, pl.ds(chunk * CHUNK, WINDOW), :]
            rows = rows.astype(BF).reshape(8 * WINDOW, frames * lanes)
            first_layer(rows, first_ref.at[which], bias1, hidden, row * (1 + chunk * CHUNK), channels)
        for strip in range(depth // 2):
            slab = hidden[pl.ds(2 * row * strip, 4 * row), :]
            mid_layer(slab, mid_ref[which], bias2, deeper, row * (1 + 2 * strip), channels, lanes)
        for chunk in range(depth // CHUNK):
            slab = deeper[pl.ds(chunk * CHUNK * row, (CHUNK + 2) * row), :]
            parts = last_layer(slab, last_ref[which], lanes)
            for half in range(2):
                for frame in range(frames):
                    base = (frame * depth + chunk * CHUNK) * stride + step
                    result[half, pl.ds(base, CHUNK, stride), :] = parts[half][:, frame * lanes : (frame + 1) * lanes]
        return 0

    lax.fori_loop(0, 2 * per, pair, 0)
    for half in range(2):
        out_ref[:, half * lanes : (half + 1) * lanes] = result[half].astype(BF)


def planes(arrived, first, mid, last, bias, frames, depth):
    rows, n = arrived.shape
    lanes = n // 2
    channels = bias.shape[2]
    per = n // (frames * depth)
    row = 2 * channels
    args = [arrived, first, mid, last, bias]
    return pl.pallas_call(
        functools.partial(planes_kernel, frames, depth, per, channels),
        out_shape=jax.ShapeDtypeStruct((rows, n), BF),
        grid=(1,),
        in_specs=[whole(a.shape) for a in args],
        out_specs=whole((rows, n)),
        scratch_shapes=[
            pltpu.VMEM((2, rows, lanes), F32),
            pltpu.VMEM((2, rows, lanes), F32),
            pltpu.VMEM((8, depth + 2 * LEAD, frames * lanes), F32),
            pltpu.VMEM((row * (depth + 2), frames * lanes), BF),
            pltpu.VMEM((row * (depth + 2), frames * lanes), BF),
        ],
        cost_estimate=cost(2 * 9 * channels * channels * 2 * n * n * 3, 4 * n * n),
        name="planes",
    )(*args)


def volume_kernel(
    channels, mine_ref, other_ref, first_ref, mid_ref, last_ref, bias_ref, after_ref, out_ref,
    window, hidden, deeper,
):
    n = mine_ref.shape[0]
    lanes = n // 2
    row = 2 * channels
    depth = n // 2
    edge = row * (depth + 1)
    zeros = jnp.zeros((8, LEAD, lanes), F32)
    window[:, 0:LEAD, :] = zeros
    window[:, pl.ds(LEAD + n, LEAD), :] = zeros
    for channel, ref in enumerate((mine_ref, other_ref)):
        even = ref[:, :lanes].astype(F32)
        odd = ref[:, lanes:].astype(F32)
        groups = [even, odd, shifted_columns(even, 1, lanes), shifted_columns(odd, 0, lanes)]
        for group in range(4):
            window[4 * channel + group, pl.ds(LEAD, n), :] = groups[group]
    bias1 = jnp.concatenate([bias_ref[0, 0]] * 2, 1)
    bias2 = jnp.concatenate([bias_ref[0, 1]] * 2, 1)

    def seam(ref):
        ref[0:row, 0:lanes] = jnp.zeros((row, lanes), BF)
        ref[pl.ds(edge, row), pl.ds(lanes, lanes)] = jnp.zeros((row, lanes), BF)
        ref[0:row, pl.ds(lanes, lanes)] = ref[pl.ds(edge - row, row), 0:lanes]
        ref[pl.ds(edge, row), 0:lanes] = ref[row : 2 * row, pl.ds(lanes, lanes)]

    def first_step(chunk, _):
        halves = [
            window[:, pl.ds(pl.multiple_of(side * depth + chunk * CHUNK, 8), WINDOW), :] for side in range(2)
        ]
        rows = jnp.concatenate(halves, 2).astype(BF).reshape(8 * WINDOW, 2 * lanes)
        base = pl.multiple_of(row * (1 + chunk * CHUNK), row)
        first_layer(rows, first_ref.at[0], bias1, hidden, base, channels)
        return 0

    lax.fori_loop(0, depth // CHUNK, first_step, 0)
    seam(hidden)

    def mid_step(step, _):
        for inner in range(4):
            strip = step * 4 + inner
            slab = hidden[pl.ds(pl.multiple_of(2 * row * strip, row), 4 * row), :]
            base = pl.multiple_of(row * (1 + 2 * strip), row)
            mid_layer(slab, mid_ref[0], bias2, deeper, base, channels, lanes)
        return 0

    lax.fori_loop(0, depth // 8, mid_step, 0)
    seam(deeper)

    def last_step(chunk, _):
        slab = deeper[pl.ds(pl.multiple_of(chunk * CHUNK * row, row), (CHUNK + 2) * row), :]
        parts = last_layer(slab, last_ref[0], lanes)
        for half in range(2):
            for side in range(2):
                base = pl.multiple_of(side * depth + chunk * CHUNK, CHUNK)
                piece = parts[half][:, side * lanes : (side + 1) * lanes]
                out_ref[pl.ds(base, CHUNK), pl.ds(half * lanes, lanes)] = piece.astype(BF)
        return 0

    lax.fori_loop(0, depth // CHUNK, last_step, 0)


def volume(mine, other, first, mid, last, bias, after):
    n = mine.shape[0]
    lanes = n // 2
    channels = bias.shape[2]
    row = 2 * channels
    args = [mine, other]
    tables = [first, mid, last, bias]
    return pl.pallas_call(
        functools.partial(volume_kernel, channels),
        out_shape=jax.ShapeDtypeStruct((n, n), BF),
        grid=(1,),
        in_specs=[whole(a.shape) for a in args]
        + [whole((1,) + t.shape[1:]) for t in tables]
        + [pl.BlockSpec(memory_space=pl.ANY)],
        out_specs=whole((n, n)),
        scratch_shapes=[
            pltpu.VMEM((8, n + 2 * LEAD, lanes), F32),
            pltpu.VMEM((row * (n // 2 + 2), n), BF),
            pltpu.VMEM((row * (n // 2 + 2), n), BF),
        ],
        cost_estimate=cost(2 * 9 * channels * channels * n * n * 3, 4 * n * n),
        name="volume",
    )(*args, *tables, after)


def combine_kernel(devices, fast, states, data, res_z, *refs):
    n = data.shape[0]
    out = refs[-1]
    split = parity_matrix(n)
    if fast:
        per = n // devices
        both = refs[0][...].astype(F32).reshape(devices, 2 * per, n)
        by_x = both[:, :per].reshape(n, n).astype(BF)
        by_y = both[:, per:].reshape(n, n).astype(BF)
    else:
        by_x, by_y = refs[0][...], refs[1][...]
    residuals = [nt(res_z[...], split), nt(split, by_x), nt(by_y, split)]
    current = [states[k] for k in range(4)]
    estimates = [data[...]] + [current[k + 1] - residuals[k] for k in range(3)]
    reflected = [2.0 * estimates[k] - current[k] for k in range(4)]
    average = (reflected[0] + reflected[1] + reflected[2] + reflected[3]) * 0.25
    for k in range(4):
        out[k] = (1.0 - relaxation) * current[k] + relaxation * (2.0 * average - reflected[k])


def combine(current, data, res_z, returned, devices):
    n = data.shape[0]
    per = n // devices
    fast = per % 8 == 0
    if fast:
        parts = [returned]
    else:
        shaped = returned.reshape(devices, 2, per, n)
        parts = [shaped[:, 0].reshape(n, n), shaped[:, 1].reshape(n, n)]
    args = [current, data, res_z] + parts
    return pl.pallas_call(
        functools.partial(combine_kernel, devices, fast),
        out_shape=jax.ShapeDtypeStruct(current.shape, F32),
        grid=(1,),
        in_specs=[whole(a.shape) for a in args],
        out_specs=whole(current.shape),
        cost_estimate=cost(6 * n**3, 40 * n * n),
        name="combine",
    )(*args)


def exchanged(rows, devices):
    n = rows.shape[1]
    blocks = rows.reshape(devices, rows.shape[0] // devices, n)
    blocks = lax.all_to_all(blocks, ("frame", "plane"), split_axis=0, concat_axis=0, tiled=True)
    return blocks.reshape(rows.shape)


def on_device(states, measured, response, kernel_in, bias_in, kernel_mid, bias_mid, kernel_out):
    frames = lax.axis_size("frame")
    depth = lax.axis_size("plane")
    devices = frames * depth
    current = states[:, 0, 0]
    mine, toward = spread(current, devices)
    other = lax.ppermute(mine, "frame", [(f, frames - 1 - f) for f in range(frames)])
    arrived = exchanged(toward, devices)
    data, first, mid, last, bias = prepare(
        current, measured[:, 0], response, kernel_in, bias_in, kernel_mid, bias_mid, kernel_out
    )
    residual = planes(arrived, first, mid, last, bias, frames, depth)
    returned = exchanged(residual, devices)
    res_z = volume(mine, other, first, mid, last, bias, residual)
    return combine(current, data, res_z, returned, devices)[:, None, None]


def solution(mesh):
    placed = (
        P(None, "frame", "plane", None, None),
        P("frame", "plane", None, None),
        P(),
        P(),
        P(),
        P(),
        P(),
        P(),
    )
    return jax.shard_map(
        on_device,
        mesh=mesh,
        in_specs=placed,
        out_specs=P(None, "frame", "plane", None, None),
        check_vma=False,
    )
```

profile of v0, /device:TPU:0, one launch (start us, length us, event | category | flops | bytes accessed | tf_op | source)
XLA Modules:
  0.0 67.1 jit_solution(9958079294786127149)
XLA Ops:
  0.0 0.0 copy-start.2
  0.0 0.0 copy-start.3
  0.0 2.1 %spread.1 = (bf16[256,256]{1,0:T(8,128)(2,1)}, bf16[512,256]{1,0:T(8,128)(2,1)}) custom-call(f32[4,256,256]{2,1,0:T(8,128)} %bitcast.18, f32[4,256,256]{2,1,0:T(8,128)} %bitcast.19, f32[4,256,256]{2,1,0:T(8,128)} %bitcast.20), custom_call_target="tpu_custom_call" | custom-call | flops 100663296 | bytes 1179648 | tf_op jit(solution)/shard_map/spread/pallas_call | solution.py:94
  2.1 7.3 %all-to-all-start = ((bf16[32,16,256]{2,1,0:T(8,128)(2,1)}), bf16[32,16,256]{2,1,0:T(8,128)(2,1)S(1)}, u32[]{:S(2)}, u32[]{:S(2)}) async-start(bf16[32,16,256]{2,1,0:T(8,128)(2,1)} %bitcast.25), calls=%async_computation | async-start | bytes 524288 | tf_op jit(solution)/shard_map/all_to_all | solution.py:496
  9.5 0.0 copy-done.2
  9.5 0.8 %copy.14.kin = bf16[3,3,32,6]{3,2,1,0:T(8,128)(2,1)} copy(bf16[3,3,32,6]{2,3,1,0:T(8,128)(2,1)S(1)} %reshape.19) | data formatting | bytes 6912 | tf_op jit(solution)/shard_map/reshape | solution.py:223
  10.3 0.0 copy-done.3
  10.3 0.6 copy.15.kout
  10.9 0.0 copy-done.4
  10.9 0.6 copy.19
  11.5 4.7 %prepare.1 = (f32[256,256]{1,0:T(8,128)}, bf16[3,1024,256]{2,1,0:T(8,128)(2,1)}, bf16[3,256,256]{2,1,0:T(8,128)(2,1)}, bf16[3,64,1152]{2,1,0:T(8,128)(2,1)}, f32[3,2,32,128]{3,2,1,0:T(8,128)}) custom-call(f32[4,256,256]{2,1,0:T(8,128)} %bitcast.21, f32[1,256,256]{2,1,0:T(8,128)} %bitcast.29, f32[256,256]{1,0:T(8,128)} %response.1, ...), custom_call_target="tpu_custom_call" | custom-call | flops 671088640 | bytes 2621440 | tf_op jit(solution)/shard_map/prepare/pallas_call | solution.py:235
  16.2 3.5 %all-to-all-done = bf16[32,16,256]{2,1,0:T(8,128)(2,1)S(1)} async-done(((bf16[32,16,256]{2,1,0:T(8,128)(2,1)}), bf16[32,16,256]{2,1,0:T(8,128)(2,1)S(1)}, u32[]{:S(2)}, u32[]{:S(2)}) %all-to-all-start) | async-done | bytes 262176 | tf_op jit(solution)/shard_map/all_to_all | solution.py:496
  19.7 0.0 copy-start.1
  19.7 0.7 %copy-done.1 = bf16[32,16,256]{2,1,0:T(8,128)(2,1)} copy-done((bf16[32,16,256]{2,1,0:T(8,128)(2,1)}, bf16[32,16,256]{2,1,0:T(8,128)(2,1)S(1)}, u32[]{:S(2)}) %copy-start.1) | copy-done | bytes 262168
  20.4 18.8 %planes.1.after_ref = bf16[512,256]{1,0:T(8,128)(2,1)} custom-call(bf16[512,256]{1,0:T(8,128)(2,1)} %bitcast.24, bf16[3,1024,256]{2,1,0:T(8,128)(2,1)} %get-tuple-element.14.first_ref, bf16[3,256,256]{2,1,0:T(8,128)(2,1)} %get-tuple-element.15.mid_ref, bf16[3,64,1152]{2,1,0:T(8,128)(2,1)} %get-tuple-element.16.last_ref, ...), custom_call_target="tpu_custom_call" | custom-call | flops 7247757312 | bytes 262144 | tf_op jit(solution)/shard_map/planes/pallas_call | solution.py:346
  39.2 2.6 %all-to-all-start.1 = ((bf16[32,16,256]{2,1,0:T(8,128)(2,1)}), bf16[32,16,256]{2,1,0:T(8,128)(2,1)S(1)}, u32[]{:S(2)}, u32[]{:S(2)}) async-start(bf16[32,16,256]{2,1,0:T(8,128)(2,1)} %bitcast.26), calls=%async_computation.1 | async-start | bytes 524288 | tf_op jit(solution)/shard_map/all_to_all | solution.py:496
  41.8 0.0 copy-done.5
  41.8 1.8 %collective-permute-start = (bf16[256,256]{1,0:T(8,128)(2,1)S(1)}, bf16[256,256]{1,0:T(8,128)(2,1)S(1)}, u32[]{:S(2)}, u32[]{:S(2)}) collective-permute-start(bf16[256,256]{1,0:T(8,128)(2,1)S(1)} %copy-done.5), channel_id=1, source_target_pairs={{0,16},{16,0},{1,17},{17,1},{2,18},{18,2},{3,19},{19,3},{4,20},{20... | collective-permute-start | bytes 393224 | tf_op jit(solution)/shard_map/ppermute | solution.py:506
  43.6 5.7 %collective-permute-done.other_ref = bf16[256,256]{1,0:T(8,128)(2,1)S(1)} collective-permute-done((bf16[256,256]{1,0:T(8,128)(2,1)S(1)}, bf16[256,256]{1,0:T(8,128)(2,1)S(1)}, u32[]{:S(2)}, u32[]{:S(2)}) %collective-permute-start) | collective-permute-done | bytes 131104 | tf_op jit(solution)/shard_map/ppermute | solution.py:506
  49.3 0.6 copy-done.6
  50.0 13.6 %volume.1.res_z = bf16[256,256]{1,0:T(8,128)(2,1)} custom-call(bf16[256,256]{1,0:T(8,128)(2,1)} %get-tuple-element.13.mine_ref, bf16[256,256]{1,0:T(8,128)(2,1)} %copy-done.6, bf16[3,1024,256]{2,1,0:T(8,128)(2,1)} %get-tuple-element.14.first_ref, bf16[3,256,256]{2,1,0:T(8,128)(2,1)} %get-tuple-element.15.mid_ref, ...), custom_call_target="tpu_custom_call" | custom-call | flops 3623878656 | bytes 262144 | tf_op jit(solution)/shard_map/volume/pallas_call | solution.py:434
  63.6 0.0 all-to-all-done.1
  63.6 0.7 %copy-done = bf16[32,16,256]{2,1,0:T(8,128)(2,1)} copy-done((bf16[32,16,256]{2,1,0:T(8,128)(2,1)}, bf16[32,16,256]{2,1,0:T(8,128)(2,1)S(1)}, u32[]{:S(2)}) %copy-start) | copy-done | bytes 262168
  64.3 2.8 %combine.1 = f32[4,256,256]{2,1,0:T(8,128)} custom-call(f32[4,256,256]{2,1,0:T(8,128)} %bitcast.22, f32[256,256]{1,0:T(8,128)} %get-tuple-element.12.data, bf16[256,256]{1,0:T(8,128)(2,1)} %volume.1.res_z, bf16[512,256]{1,0:T(8,128)(2,1)} %bitcast.23), custom_call_target="tpu_custom_call" | custom-call | flops 100663296 | bytes 2621440 | tf_op jit(solution)/shard_map/combine/pallas_call | solution.py:482
  (5 shorter events, 0.0 us)
Async XLA Ops:
  0.0 9.5 %copy-start.2 = (bf16[3,9,32,2]{2,3,1,0:T(2,128)(2,1)S(1)}, bf16[3,9,32,2]{2,3,1,0:T(2,128)(2,1)}, u32[]{:S(2)}) copy-start(bf16[3,9,32,2]{2,3,1,0:T(2,128)(2,1)} %param.13) | copy-start | bytes 10372
  0.0 10.3 %copy-start.3 = (bf16[3,9,32]{2,0,1:T(4,128)(2,1)S(1)}, bf16[3,9,32]{2,0,1:T(4,128)(2,1)}, u32[]{:S(2)}) copy-start(bf16[3,9,32]{2,0,1:T(4,128)(2,1)} %param.17) | copy-start | bytes 5188
  0.0 10.9 %copy-start.4 = (f32[3,1,32]{2,1,0:T(1,128)S(1)}, f32[3,1,32]{2,1,0:T(1,128)}, u32[]{:S(2)}) copy-start(f32[3,1,32]{2,1,0:T(1,128)} %param.16) | copy-start | bytes 1156
  2.1 17.6 %all-to-all-start = ((bf16[32,16,256]{2,1,0:T(8,128)(2,1)}), bf16[32,16,256]{2,1,0:T(8,128)(2,1)S(1)}, u32[]{:S(2)}, u32[]{:S(2)}) async-start(bf16[32,16,256]{2,1,0:T(8,128)(2,1)} %bitcast.25), calls=%async_computation | async-start | bytes 524288 | tf_op jit(solution)/shard_map/all_to_all | solution.py:496
  19.7 0.7 %copy-start.1 = (bf16[32,16,256]{2,1,0:T(8,128)(2,1)}, bf16[32,16,256]{2,1,0:T(8,128)(2,1)S(1)}, u32[]{:S(2)}) copy-start(bf16[32,16,256]{2,1,0:T(8,128)(2,1)S(1)} %all-to-all-done) | copy-start | bytes 786436
  20.4 21.4 %copy-start.5 = (bf16[256,256]{1,0:T(8,128)(2,1)S(1)}, bf16[256,256]{1,0:T(8,128)(2,1)}, u32[]{:S(2)}) copy-start(bf16[256,256]{1,0:T(8,128)(2,1)} %get-tuple-element.13.mine_ref) | copy-start | bytes 393220
  39.2 24.4 %all-to-all-start.1 = ((bf16[32,16,256]{2,1,0:T(8,128)(2,1)}), bf16[32,16,256]{2,1,0:T(8,128)(2,1)S(1)}, u32[]{:S(2)}, u32[]{:S(2)}) async-start(bf16[32,16,256]{2,1,0:T(8,128)(2,1)} %bitcast.26), calls=%async_computation.1 | async-start | bytes 524288 | tf_op jit(solution)/shard_map/all_to_all | solution.py:496
  41.8 7.5 %collective-permute-start = (bf16[256,256]{1,0:T(8,128)(2,1)S(1)}, bf16[256,256]{1,0:T(8,128)(2,1)S(1)}, u32[]{:S(2)}, u32[]{:S(2)}) collective-permute-start(bf16[256,256]{1,0:T(8,128)(2,1)S(1)} %copy-done.5), channel_id=1, source_target_pairs={{0,16},{16,0},{1,17},{17,1},{2,18},{18,2},{3,19},{19,3},{4,20},{20... | collective-permute-start | bytes 393224 | tf_op jit(solution)/shard_map/ppermute | solution.py:506
  49.3 0.6 copy-start.6
  63.6 0.7 %copy-start = (bf16[32,16,256]{2,1,0:T(8,128)(2,1)}, bf16[32,16,256]{2,1,0:T(8,128)(2,1)S(1)}, u32[]{:S(2)}) copy-start(bf16[32,16,256]{2,1,0:T(8,128)(2,1)S(1)} %all-to-all-done.1) | copy-start | bytes 786436
where the time goes:
time: 67.5 us; the launch traced here: 67.1 us
  Pallas kernels  42.1 us (62%)
  starting transfers between devices  11.7 us (17%)
  waiting for transfers between devices  9.28 us (14%)
  local copies, waits for them, and re-layouts  4.03 us (6%)
    pallas_call x1, Pallas kernels, planes(): pl.pallas_call(functools.partial(planes_kernel, frames, depth, per, chann...  18.8 us
    pallas_call x1, Pallas kernels, volume(): pl.pallas_call(functools.partial(volume_kernel, channels), out_shape=jax....  13.6 us
    all_to_all x2, starting transfers between devices, exchanged(): lax.all_to_all(blocks, ('frame', 'plane'), split_axis=0, concat_axis=0, t...  9.91 us
    ppermute x1, waiting for transfers between devices, on_device(): lax.ppermute(mine, 'frame', [(f, frames - 1 - f) for f in range(frames)])  5.74 us
    pallas_call x1, Pallas kernels, prepare(): pl.pallas_call(prepare_kernel, out_shape=shapes, grid=(1,), in_specs=[age...  4.73 us
    all_to_all x2, waiting for transfers between devices, exchanged(): lax.all_to_all(blocks, ('frame', 'plane'), split_axis=0, concat_axis=0, t...  3.54 us
    unnamed x16, local copies, waits for them, and re-layouts  3.24 us
    pallas_call x1, Pallas kernels, combine(): pl.pallas_call(functools.partial(combine_kernel, devices, fast), out_shap...  2.85 us
  transfers between devices with their start and end apart: 3, of which 2 were waited for; matrix products, arithmetic and copies ran while one was open for 3% of the time, Pallas kernels for 27%

commit v1 on v0

--- a/solution.py
+++ b/solution.py
@@ -15,8 +15,9 @@
 F32 = jnp.float32
 
 CHUNK = 16
-WINDOW = 32
-LEAD = 8
+FIRST = 8
+WINDOW = 16
+LEAD = 4
 
 FIRST_TAP = {(0, 3): 0, (0, 0): 1, (0, 1): 2, (1, 0): 0, (1, 1): 1, (1, 2): 2}
 LATER_TAP = {
@@ -125,7 +126,7 @@
         for p in range(3):
             vectors[parity, p] = mm(taps[p], pick)
     pieces = []
-    for row in range(CHUNK):
+    for row in range(FIRST):
         for parity in range(2):
             piece = jnp.zeros((channels, wide), F32)
             for p in range(3):
@@ -140,9 +141,9 @@
     repeat = (iota((channels, wide), 0) == iota((channels, wide), 1) % channels).astype(F32).astype(BF)
     spread_taps = mm(taps, repeat)
     pieces = []
-    for shifted in range(2):
-        for row in range(2):
-            for parity in range(2):
+    for row in range(2):
+        for parity in range(2):
+            for shifted in range(2):
                 piece = jnp.zeros((channels, wide), F32)
                 for p in range(3):
                     for source in range(2):
@@ -226,7 +227,7 @@
     wide = (CHUNK + 2) * 2 * channels
     shapes = [
         jax.ShapeDtypeStruct((n, n), F32),
-        jax.ShapeDtypeStruct((3, CHUNK * 2 * channels, 8 * WINDOW), BF),
+        jax.ShapeDtypeStruct((3, FIRST * 2 * channels, 8 * WINDOW), BF),
         jax.ShapeDtypeStruct((3, 8 * channels, 8 * channels), BF),
         jax.ShapeDtypeStruct((3, 4 * CHUNK, wide), BF),
         jax.ShapeDtypeStruct((3, 2, channels, lanes), F32),
@@ -262,7 +263,7 @@
 
 def first_layer(window, weights, bias, hidden_ref, base, channels):
     step = 8 * channels
-    for index in range(CHUNK * 2 * channels // step):
+    for index in range(FIRST * 2 * channels // step):
         product = mm(weights[pl.ds(index * step, step), :], window)
         for part in range(step // channels):
             piece = product[part * channels : (part + 1) * channels] + bias
@@ -272,8 +273,8 @@
 def mid_layer(slab, weights, bias, out_ref, base, channels, lanes):
     product = mm(weights, slab)
     for part in range(4):
-        kept = product[part * channels : (part + 1) * channels]
-        moved = product[(4 + part) * channels : (5 + part) * channels]
+        kept = product[2 * part * channels : (2 * part + 1) * channels]
+        moved = product[(2 * part + 1) * channels : (2 * part + 2) * channels]
         piece = kept + shifted_columns(moved, part % 2, lanes) + bias
         out_ref[pl.ds(base + part * channels, channels), :] = halve(piece)
 
@@ -289,7 +290,7 @@
 
 def planes_kernel(
     frames, depth, per, channels,
-    arrived_ref, first_ref, mid_ref, last_ref, bias_ref, out_ref,
+    arrived_ref, first_ref, mid_ref, last_ref, bias_ref, after_ref, out_ref,
     source, result, window, hidden, deeper,
 ):
     lanes = arrived_ref.shape[1] // 2
@@ -299,44 +300,50 @@
         source[half] = arrived_ref[:, half * lanes : (half + 1) * lanes].astype(F32)
     window[...] = jnp.zeros_like(window)
     for ref in (hidden, deeper):
-        ref[0:row, :] = jnp.zeros((row, frames * lanes), BF)
-        ref[pl.ds(row * (depth + 1), row), :] = jnp.zeros((row, frames * lanes), BF)
-
-    def pair(step, _):
-        which = step // per + 1
-        for frame in range(frames):
-            base = frame * depth * stride + step
-            even = source[0, pl.ds(base, depth, stride), :]
-            odd = source[1, pl.ds(base, depth, stride), :]
-            groups = [even, odd, shifted_columns(even, 1, lanes), shifted_columns(odd, 0, lanes)]
-            for image in range(frames):
-                channel = (frame - image) % frames
-                for group in range(4):
-                    window[4 * channel + group, pl.ds(LEAD, depth), pl.ds(image * lanes, lanes)] = groups[group]
-        bias1 = jnp.concatenate([bias_ref[which, 0]] * frames, 1)
-        bias2 = jnp.concatenate([bias_ref[which, 1]] * frames, 1)
+        for k in range(2):
+            ref[k, 0:row, :] = jnp.zeros((row, frames * lanes), BF)
+            ref[k, pl.ds(row * (depth + 1), row), :] = jnp.zeros((row, frames * lanes), BF)
+
+    bias1 = [jnp.concatenate([bias_ref[k + 1, 0]] * frames, 1) for k in range(2)]
+    bias2 = [jnp.concatenate([bias_ref[k + 1, 1]] * frames, 1) for k in range(2)]
+
+    def pairs(plane, _):
+        for k in range(2):
+            for frame in range(frames):
+                base = frame * depth * stride + k * per + plane
+                even = source[0, pl.ds(base, depth, stride), :]
+                odd = source[1, pl.ds(base, depth, stride), :]
+                groups = [even, odd, shifted_columns(even, 1, lanes), shifted_columns(odd, 0, lanes)]
+                for image in range(frames):
+                    channel = (frame - image) % frames
+                    for group in range(4):
+                        window[k, 4 * channel + group, pl.ds(LEAD, depth), pl.ds(image * lanes, lanes)] = groups[group]
+        for chunk in range(depth // FIRST):
+            for k in range(2):
+                rows = window[k, :, pl.ds(chunk * FIRST, WINDOW), :]
+                rows = rows.astype(BF).reshape(8 * WINDOW, frames * lanes)
+                first_layer(rows, first_ref.at[k + 1], bias1[k], hidden.at[k], row * (1 + chunk * FIRST), channels)
+        for strip in range(depth // 2):
+            for k in range(2):
+                slab = hidden[k, pl.ds(2 * row * strip, 4 * row), :]
+                mid_layer(slab, mid_ref[k + 1], bias2[k], deeper.at[k], row * (1 + 2 * strip), channels, lanes)
         for chunk in range(depth // CHUNK):
-            rows = window[:, pl.ds(chunk * CHUNK, WINDOW), :]
-            rows = rows.astype(BF).reshape(8 * WINDOW, frames * lanes)
-            first_layer(rows, first_ref.at[which], bias1, hidden, row * (1 + chunk * CHUNK), channels)
-        for strip in range(depth // 2):
-            slab = hidden[pl.ds(2 * row * strip, 4 * row), :]
-            mid_layer(slab, mid_ref[which], bias2, deeper, row * (1 + 2 * strip), channels, lanes)
-        for chunk in range(depth // CHUNK):
-            slab = deeper[pl.ds(chunk * CHUNK * row, (CHUNK + 2) * row), :]
-            parts = last_layer(slab, last_ref[which], lanes)
-            for half in range(2):
-                for frame in range(frames):
-                    base = (frame * depth + chunk * CHUNK) * stride + step
-                    result[half, pl.ds(base, CHUNK, stride), :] = parts[half][:, frame * lanes : (frame + 1) * lanes]
+            for k in range(2):
+                slab = deeper[k, pl.ds(chunk * CHUNK * row, (CHUNK + 2) * row), :]
+                parts = last_layer(slab, last_ref[k + 1], lanes)
+                for half in range(2):
+                    for frame in range(frames):
+                        base = (frame * depth + chunk * CHUNK) * stride + k * per + plane
+                        piece = parts[half][:, frame * lanes : (frame + 1) * lanes]
+                        result[half, pl.ds(base, CHUNK, stride), :] = piece
         return 0
 
-    lax.fori_loop(0, 2 * per, pair, 0)
+    lax.fori_loop(0, per, pairs, 0)
     for half in range(2):
         out_ref[:, half * lanes : (half + 1) * lanes] = result[half].astype(BF)
 
 
-def planes(arrived, first, mid, last, bias, frames, depth):
+def planes(arrived, first, mid, last, bias, after, frames, depth):
     rows, n = arrived.shape
     lanes = n // 2
     channels = bias.shape[2]
@@ -347,18 +354,18 @@
         functools.partial(planes_kernel, frames, depth, per, channels),
         out_shape=jax.ShapeDtypeStruct((rows, n), BF),
         grid=(1,),
-        in_specs=[whole(a.shape) for a in args],
+        in_specs=[whole(a.shape) for a in args] + [pl.BlockSpec(memory_space=pl.ANY)],
         out_specs=whole((rows, n)),
         scratch_shapes=[
             pltpu.VMEM((2, rows, lanes), F32),
             pltpu.VMEM((2, rows, lanes), F32),
-            pltpu.VMEM((8, depth + 2 * LEAD, frames * lanes), F32),
-            pltpu.VMEM((row * (depth + 2), frames * lanes), BF),
-            pltpu.VMEM((row * (depth + 2), frames * lanes), BF),
+            pltpu.VMEM((2, 8, depth + 2 * LEAD, frames * lanes), F32),
+            pltpu.VMEM((2, row * (depth + 2), frames * lanes), BF),
+            pltpu.VMEM((2, row * (depth + 2), frames * lanes), BF),
         ],
         cost_estimate=cost(2 * 9 * channels * channels * 2 * n * n * 3, 4 * n * n),
         name="planes",
-    )(*args)
+    )(*args, after)
 
 
 def volume_kernel(
@@ -388,30 +395,34 @@
         ref[0:row, pl.ds(lanes, lanes)] = ref[pl.ds(edge - row, row), 0:lanes]
         ref[pl.ds(edge, row), 0:lanes] = ref[row : 2 * row, pl.ds(lanes, lanes)]
 
-    def first_step(chunk, _):
+    def first_chunk(chunk):
         halves = [
-            window[:, pl.ds(pl.multiple_of(side * depth + chunk * CHUNK, 8), WINDOW), :] for side in range(2)
+            window[:, pl.ds(pl.multiple_of(side * depth + chunk * FIRST, 8), WINDOW), :] for side in range(2)
         ]
         rows = jnp.concatenate(halves, 2).astype(BF).reshape(8 * WINDOW, 2 * lanes)
-        base = pl.multiple_of(row * (1 + chunk * CHUNK), row)
+        base = pl.multiple_of(row * (1 + chunk * FIRST), row)
         first_layer(rows, first_ref.at[0], bias1, hidden, base, channels)
+
+    def first_step(step, _):
+        for inner in range(4):
+            first_chunk(step * 4 + inner)
         return 0
 
-    lax.fori_loop(0, depth // CHUNK, first_step, 0)
+    lax.fori_loop(0, depth // (4 * FIRST), first_step, 0)
     seam(hidden)
 
     def mid_step(step, _):
-        for inner in range(4):
-            strip = step * 4 + inner
+        for inner in range(16):
+            strip = step * 16 + inner
             slab = hidden[pl.ds(pl.multiple_of(2 * row * strip, row), 4 * row), :]
             base = pl.multiple_of(row * (1 + 2 * strip), row)
             mid_layer(slab, mid_ref[0], bias2, deeper, base, channels, lanes)
         return 0
 
-    lax.fori_loop(0, depth // 8, mid_step, 0)
+    lax.fori_loop(0, depth // 32, mid_step, 0)
     seam(deeper)
 
-    def last_step(chunk, _):
+    def last_chunk(chunk):
         slab = deeper[pl.ds(pl.multiple_of(chunk * CHUNK * row, row), (CHUNK + 2) * row), :]
         parts = last_layer(slab, last_ref[0], lanes)
         for half in range(2):
@@ -419,9 +430,13 @@
                 base = pl.multiple_of(side * depth + chunk * CHUNK, CHUNK)
                 piece = parts[half][:, side * lanes : (side + 1) * lanes]
                 out_ref[pl.ds(base, CHUNK), pl.ds(half * lanes, lanes)] = piece.astype(BF)
+
+    def last_step(step, _):
+        for inner in range(4):
+            last_chunk(step * 4 + inner)
         return 0
 
-    lax.fori_loop(0, depth // CHUNK, last_step, 0)
+    lax.fori_loop(0, depth // (4 * CHUNK), last_step, 0)
 
 
 def volume(mine, other, first, mid, last, bias, after):
@@ -508,7 +523,7 @@
     data, first, mid, last, bias = prepare(
         current, measured[:, 0], response, kernel_in, bias_in, kernel_mid, bias_mid, kernel_out
     )
-    residual = planes(arrived, first, mid, last, bias, frames, depth)
+    residual = planes(arrived, first, mid, last, bias, other, frames, depth)
     returned = exchanged(residual, devices)
     res_z = volume(mine, other, first, mid, last, bias, residual)
     return combine(current, data, res_z, returned, devices)[:, None, None]

time: 67.5 us -> 50.7 us (0.75)
  Pallas kernels: 42.1 us -> 30.2 us
  waiting for transfers between devices: 9.28 us -> 4.76 us
    ppermute x1, waiting for transfers between devices: 5.74 us -> 0.01 us  [on_device(): lax.ppermute(mine, 'frame', [(f, frames - 1 - f) for f in range(frames)])]
    pallas_call x1, Pallas kernels: 13.6 us -> 8.14 us  [volume(): pl.pallas_call(functools.partial(volume_kernel, channels), out_shape=jax....]
    pallas_call x1, Pallas kernels: 18.8 us -> 13.4 us  [planes(): pl.pallas_call(functools.partial(planes_kernel, frames, depth, per, chann...]
    all_to_all x2, waiting for transfers between devices: 3.54 us -> 4.76 us  [exchanged(): lax.all_to_all(blocks, ('frame', 'plane'), split_axis=0, concat_axis=0, t...]
    pallas_call x1, Pallas kernels: 4.73 us -> 3.75 us  [prepare(): pl.pallas_call(prepare_kernel, out_shape=shapes, grid=(1,), in_specs=[age...]
  transfers between devices with their start and end apart: 3 -> 3, of which waited for: 2 -> 2; matrix products, arithmetic and copies ran while one was open for 3% -> 4% of each run, Pallas kernels for 27% -> 24%
where the time goes in v1:
time: 50.7 us; the launch traced here: 50.3 us
  Pallas kernels  30.2 us (60%)
  starting transfers between devices  11.9 us (23%)
  waiting for transfers between devices  4.76 us (9%)
  local copies, waits for them, and re-layouts  3.41 us (7%)
    pallas_call x1, Pallas kernels, planes(): pl.pallas_call(functools.partial(planes_kernel, frames, depth, per, chann...  13.4 us
    all_to_all x2, starting transfers between devices, exchanged(): lax.all_to_all(blocks, ('frame', 'plane'), split_axis=0, concat_axis=0, t...  10.1 us
    pallas_call x1, Pallas kernels, volume(): pl.pallas_call(functools.partial(volume_kernel, channels), out_shape=jax....  8.14 us
    all_to_all x2, waiting for transfers between devices, exchanged(): lax.all_to_all(blocks, ('frame', 'plane'), split_axis=0, concat_axis=0, t...  4.76 us
    pallas_call x1, Pallas kernels, prepare(): pl.pallas_call(prepare_kernel, out_shape=shapes, grid=(1,), in_specs=[age...  3.75 us
    pallas_call x1, Pallas kernels, combine(): pl.pallas_call(functools.partial(combine_kernel, devices, fast), out_shap...  2.84 us
    unnamed x16, local copies, waits for them, and re-layouts  2.6 us
    pallas_call x1, Pallas kernels, spread(): pl.pallas_call(functools.partial(spread_kernel, devices, fast), out_shape...  2.1 us
  transfers between devices with their start and end apart: 3, of which 2 were waited for; matrix products, arithmetic and copies ran while one was open for 4% of the time, Pallas kernels for 24%

profile of v1, /device:TPU:0, one launch (start us, length us, event | category | flops | bytes accessed | tf_op | source)
XLA Modules:
  0.0 50.3 jit_solution(8518687628906419446)
XLA Ops:
  0.0 2.1 %spread.1 = (bf16[256,256]{1,0:T(8,128)(2,1)}, bf16[512,256]{1,0:T(8,128)(2,1)}) custom-call(f32[4,256,256]{2,1,0:T(8,128)} %bitcast.18, f32[4,256,256]{2,1,0:T(8,128)} %bitcast.19, f32[4,256,256]{2,1,0:T(8,128)} %bitcast.20), custom_call_target="tpu_custom_call" | custom-call | flops 100663296 | bytes 1179648 | tf_op jit(solution)/shard_map/spread/pallas_call | solution.py:95
  2.1 0.0 copy-start.5
  2.1 7.3 %all-to-all-start = ((bf16[32,16,256]{2,1,0:T(8,128)(2,1)}), bf16[32,16,256]{2,1,0:T(8,128)(2,1)S(1)}, u32[]{:S(2)}, u32[]{:S(2)}) async-start(bf16[32,16,256]{2,1,0:T(8,128)(2,1)} %bitcast.25), calls=%async_computation | async-start | bytes 524288 | tf_op jit(solution)/shard_map/all_to_all | solution.py:511
  9.4 0.0 copy-start.4
  9.4 0.0 copy-done.5
  9.5 0.0 copy-start.2
  9.5 1.8 %collective-permute-start = (bf16[256,256]{1,0:T(8,128)(2,1)S(1)}, bf16[256,256]{1,0:T(8,128)(2,1)S(1)}, u32[]{:S(2)}, u32[]{:S(2)}) collective-permute-start(bf16[256,256]{1,0:T(8,128)(2,1)S(1)} %copy-done.5), channel_id=1, source_target_pairs={{0,16},{16,0},{1,17},{17,1},{2,18},{18,2},{3,19},{19,3},{4,20},{20... | collective-permute-start | bytes 393224 | tf_op jit(solution)/shard_map/ppermute | solution.py:521
  11.3 0.0 copy-done.4
  11.3 0.6 %copy.19 = f32[3,1,32]{2,0,1:T(4,128)} copy(f32[3,1,32]{2,1,0:T(1,128)S(1)} %copy-done.4) | data formatting | bytes 768
  11.9 0.0 copy-done.3
  11.9 0.6 %copy.15.kout = bf16[3,9,32]{2,1,0:T(8,128)(2,1)} copy(bf16[3,9,32]{2,0,1:T(4,128)(2,1)S(1)} %copy-done.3) | data formatting | bytes 3456 | tf_op args[7]
  12.5 0.0 copy-done.2
  12.5 0.8 %copy.14.kin = bf16[3,3,32,6]{3,2,1,0:T(8,128)(2,1)} copy(bf16[3,3,32,6]{2,3,1,0:T(8,128)(2,1)S(1)} %reshape.19) | data formatting | bytes 6912 | tf_op jit(solution)/shard_map/reshape | solution.py:224
  13.3 3.8 %prepare.1 = (f32[256,256]{1,0:T(8,128)}, bf16[3,512,128]{2,1,0:T(8,128)(2,1)}, bf16[3,256,256]{2,1,0:T(8,128)(2,1)}, bf16[3,64,1152]{2,1,0:T(8,128)(2,1)}, f32[3,2,32,128]{3,2,1,0:T(8,128)}) custom-call(f32[4,256,256]{2,1,0:T(8,128)} %bitcast.21, f32[1,256,256]{2,1,0:T(8,128)} %bitcast.29, f32[256,256]{1,0:T(8,128)} %response.1, ...), custom_call_target="tpu_custom_call" | custom-call | flops 671088640 | bytes 2621440 | tf_op jit(solution)/shard_map/prepare/pallas_call | solution.py:236
  17.1 0.0 collective-permute-done.after_ref.other_ref
  17.1 2.6 %all-to-all-done = bf16[32,16,256]{2,1,0:T(8,128)(2,1)S(1)} async-done(((bf16[32,16,256]{2,1,0:T(8,128)(2,1)}), bf16[32,16,256]{2,1,0:T(8,128)(2,1)S(1)}, u32[]{:S(2)}, u32[]{:S(2)}) %all-to-all-start) | async-done | bytes 262176 | tf_op jit(solution)/shard_map/all_to_all | solution.py:511
  19.7 0.0 copy-done.6
  19.7 0.7 %copy-done.1 = bf16[32,16,256]{2,1,0:T(8,128)(2,1)} copy-done((bf16[32,16,256]{2,1,0:T(8,128)(2,1)}, bf16[32,16,256]{2,1,0:T(8,128)(2,1)S(1)}, u32[]{:S(2)}) %copy-start.1) | copy-done | bytes 262168
  20.4 13.4 %planes.1.after_ref = bf16[512,256]{1,0:T(8,128)(2,1)} custom-call(bf16[512,256]{1,0:T(8,128)(2,1)} %bitcast.24, bf16[3,512,128]{2,1,0:T(8,128)(2,1)} %get-tuple-element.14.first_ref, bf16[3,256,256]{2,1,0:T(8,128)(2,1)} %get-tuple-element.15.mid_ref, bf16[3,64,1152]{2,1,0:T(8,128)(2,1)} %get-tuple-element.16.last_ref, ...), custom_call_target="tpu_custom_call" | custom-call | flops 7247757312 | bytes 262144 | tf_op jit(solution)/shard_map/planes/pallas_call | solution.py:353
  33.8 2.8 %all-to-all-start.1 = ((bf16[32,16,256]{2,1,0:T(8,128)(2,1)}), bf16[32,16,256]{2,1,0:T(8,128)(2,1)S(1)}, u32[]{:S(2)}, u32[]{:S(2)}) async-start(bf16[32,16,256]{2,1,0:T(8,128)(2,1)} %bitcast.26), calls=%async_computation.1 | async-start | bytes 524288 | tf_op jit(solution)/shard_map/all_to_all | solution.py:511
  36.5 8.1 %volume.1.res_z = bf16[256,256]{1,0:T(8,128)(2,1)} custom-call(bf16[256,256]{1,0:T(8,128)(2,1)} %get-tuple-element.13.mine_ref, bf16[256,256]{1,0:T(8,128)(2,1)} %copy-done.6, bf16[3,512,128]{2,1,0:T(8,128)(2,1)} %get-tuple-element.14.first_ref, bf16[3,256,256]{2,1,0:T(8,128)(2,1)} %get-tuple-element.15.mid_ref, ...), custom_call_target="tpu_custom_call" | custom-call | flops 3623878656 | bytes 262144 | tf_op jit(solution)/shard_map/volume/pallas_call | solution.py:449
  44.7 2.1 %all-to-all-done.1 = bf16[32,16,256]{2,1,0:T(8,128)(2,1)S(1)} async-done(((bf16[32,16,256]{2,1,0:T(8,128)(2,1)}), bf16[32,16,256]{2,1,0:T(8,128)(2,1)S(1)}, u32[]{:S(2)}, u32[]{:S(2)}) %all-to-all-start.1) | async-done | bytes 262176 | tf_op jit(solution)/shard_map/all_to_all | solution.py:511
  46.8 0.7 %copy-done = bf16[32,16,256]{2,1,0:T(8,128)(2,1)} copy-done((bf16[32,16,256]{2,1,0:T(8,128)(2,1)}, bf16[32,16,256]{2,1,0:T(8,128)(2,1)S(1)}, u32[]{:S(2)}) %copy-start) | copy-done | bytes 262168
  47.5 2.8 %combine.1 = f32[4,256,256]{2,1,0:T(8,128)} custom-call(f32[4,256,256]{2,1,0:T(8,128)} %bitcast.22, f32[256,256]{1,0:T(8,128)} %get-tuple-element.12.data, bf16[256,256]{1,0:T(8,128)(2,1)} %volume.1.res_z, bf16[512,256]{1,0:T(8,128)(2,1)} %bitcast.23), custom_call_target="tpu_custom_call" | custom-call | flops 100663296 | bytes 2621440 | tf_op jit(solution)/shard_map/combine/pallas_call | solution.py:497
  (5 shorter events, 0.0 us)
Async XLA Ops:
  2.1 7.4 %copy-start.5 = (bf16[256,256]{1,0:T(8,128)(2,1)S(1)}, bf16[256,256]{1,0:T(8,128)(2,1)}, u32[]{:S(2)}) copy-start(bf16[256,256]{1,0:T(8,128)(2,1)} %get-tuple-element.13.mine_ref) | copy-start | bytes 393220
  2.1 9.8 %copy-start.3 = (bf16[3,9,32]{2,0,1:T(4,128)(2,1)S(1)}, bf16[3,9,32]{2,0,1:T(4,128)(2,1)}, u32[]{:S(2)}) copy-start(bf16[3,9,32]{2,0,1:T(4,128)(2,1)} %param.17) | copy-start | bytes 5188
  2.1 17.6 %all-to-all-start = ((bf16[32,16,256]{2,1,0:T(8,128)(2,1)}), bf16[32,16,256]{2,1,0:T(8,128)(2,1)S(1)}, u32[]{:S(2)}, u32[]{:S(2)}) async-start(bf16[32,16,256]{2,1,0:T(8,128)(2,1)} %bitcast.25), calls=%async_computation | async-start | bytes 524288 | tf_op jit(solution)/shard_map/all_to_all | solution.py:511
  9.4 1.9 %copy-start.4 = (f32[3,1,32]{2,1,0:T(1,128)S(1)}, f32[3,1,32]{2,1,0:T(1,128)}, u32[]{:S(2)}) copy-start(f32[3,1,32]{2,1,0:T(1,128)} %param.16) | copy-start | bytes 1156
  9.5 3.0 %copy-start.2 = (bf16[3,9,32,2]{2,3,1,0:T(2,128)(2,1)S(1)}, bf16[3,9,32,2]{2,3,1,0:T(2,128)(2,1)}, u32[]{:S(2)}) copy-start(bf16[3,9,32,2]{2,3,1,0:T(2,128)(2,1)} %param.13) | copy-start | bytes 10372
  9.5 7.6 %collective-permute-start = (bf16[256,256]{1,0:T(8,128)(2,1)S(1)}, bf16[256,256]{1,0:T(8,128)(2,1)S(1)}, u32[]{:S(2)}, u32[]{:S(2)}) collective-permute-start(bf16[256,256]{1,0:T(8,128)(2,1)S(1)} %copy-done.5), channel_id=1, source_target_pairs={{0,16},{16,0},{1,17},{17,1},{2,18},{18,2},{3,19},{19,3},{4,20},{20... | collective-permute-start | bytes 393224 | tf_op jit(solution)/shard_map/ppermute | solution.py:521
  17.1 2.6 %copy-start.6 = (bf16[256,256]{1,0:T(8,128)(2,1)}, bf16[256,256]{1,0:T(8,128)(2,1)S(1)}, u32[]{:S(2)}) copy-start(bf16[256,256]{1,0:T(8,128)(2,1)S(1)} %collective-permute-done.after_ref.other_ref) | copy-start | bytes 393220
  19.7 0.7 %copy-start.1 = (bf16[32,16,256]{2,1,0:T(8,128)(2,1)}, bf16[32,16,256]{2,1,0:T(8,128)(2,1)S(1)}, u32[]{:S(2)}) copy-start(bf16[32,16,256]{2,1,0:T(8,128)(2,1)S(1)} %all-to-all-done) | copy-start | bytes 786436
  33.8 13.1 %all-to-all-start.1 = ((bf16[32,16,256]{2,1,0:T(8,128)(2,1)}), bf16[32,16,256]{2,1,0:T(8,128)(2,1)S(1)}, u32[]{:S(2)}, u32[]{:S(2)}) async-start(bf16[32,16,256]{2,1,0:T(8,128)(2,1)} %bitcast.26), calls=%async_computation.1 | async-start | bytes 524288 | tf_op jit(solution)/shard_map/all_to_all | solution.py:511
  46.8 0.7 %copy-start = (bf16[32,16,256]{2,1,0:T(8,128)(2,1)}, bf16[32,16,256]{2,1,0:T(8,128)(2,1)S(1)}, u32[]{:S(2)}) copy-start(bf16[32,16,256]{2,1,0:T(8,128)(2,1)S(1)} %all-to-all-done.1) | copy-start | bytes 786436

commit v2 on v1

--- a/solution.py
+++ b/solution.py
@@ -56,25 +56,27 @@
     return (row == natural).astype(F32).astype(BF)
 
 
-def whole(shape):
-    zeros = (0,) * len(shape)
-    return pl.BlockSpec(shape, lambda i: zeros)
-
-
-def agent(k, n):
-    return pl.BlockSpec((1, n, n), lambda i: (k, 0, 0))
+VM = pl.BlockSpec(memory_space=pltpu.VMEM)
+ANYWHERE = pl.BlockSpec(memory_space=pl.ANY)
+FAR = pl.BlockSpec(memory_space=pltpu.HBM)
+PARAMS = pltpu.CompilerParams(vmem_limit_bytes=24 << 20)
 
 
 def cost(flops, moved):
     return pl.CostEstimate(flops=flops, bytes_accessed=moved, transcendentals=0)
 
 
-def spread_kernel(devices, fast, w1, w2, w3, z_ref, *outs):
-    n = w1.shape[1]
+def spread_kernel(devices, fast, states, z_ref, *rest):
+    outs, (buffer, arrival) = rest[:-2], rest[-2:]
+    n = z_ref.shape[0]
+    copies = [pltpu.make_async_copy(states.at[k + 1], buffer.at[k], arrival.at[k]) for k in range(3)]
+    for k in (1, 2, 0):
+        copies[k].start()
     split = parity_matrix(n)
-    z_ref[...] = mm(w1[0].astype(BF), split).astype(BF)
-    toward_x = tn(w2[0].astype(BF), split)
-    toward_y = mm(w3[0].astype(BF), split)
+    copies[1].wait()
+    toward_x = tn(buffer[1].astype(BF), split)
+    copies[2].wait()
+    toward_y = mm(buffer[2].astype(BF), split)
     if fast:
         per = n // devices
         both = jnp.concatenate(
@@ -84,6 +86,8 @@
     else:
         outs[0][...] = toward_x.astype(BF)
         outs[1][...] = toward_y.astype(BF)
+    copies[0].wait()
+    z_ref[...] = mm(buffer[0].astype(BF), split).astype(BF)
 
 
 def spread(current, devices):
@@ -95,12 +99,13 @@
     outs = pl.pallas_call(
         functools.partial(spread_kernel, devices, fast),
         out_shape=shapes,
-        grid=(1,),
-        in_specs=[agent(1, n), agent(2, n), agent(3, n)],
-        out_specs=[whole(s.shape) for s in shapes],
+        in_specs=[FAR],
+        out_specs=[VM] * len(shapes),
+        scratch_shapes=[pltpu.VMEM((3, n, n), F32), pltpu.SemaphoreType.DMA((3,))],
+        compiler_params=PARAMS,
         cost_estimate=cost(6 * n**3, 18 * n * n),
         name="spread",
-    )(current, current, current)
+    )(current)
     if fast:
         return outs[0], outs[1]
     parts = [o.reshape(devices, per, n) for o in outs[1:]]
@@ -189,15 +194,18 @@
 
 
 def prepare_kernel(
-    w0, measured, response, cos_ref, sin_ref, kin, bin_, kmid, bmid, kout,
-    data_ref, first_ref, mid_ref, last_ref, bias_ref,
+    states, measured, response, cos_ref, sin_ref, kin, bin_, kmid, bmid, kout,
+    data_ref, first_ref, mid_ref, last_ref, bias_ref, w0, arrival,
 ):
+    copy = pltpu.make_async_copy(states.at[0], w0, arrival)
+    copy.start()
     n = response.shape[0]
     channels = kmid.shape[2]
     lanes = bias_ref.shape[3]
     cosine, sines = cos_ref[...], sin_ref[...]
     gain = 1.0 / (1.0 + response[...])
-    source = (measured[0] + w0[0]).astype(BF)
+    copy.wait()
+    source = (measured[0] + w0[...]).astype(BF)
     row_real = mm(source, cosine).astype(BF)
     row_imag = (-mm(source, sines)).astype(BF)
     spec_real = ((mm(cosine, row_real) + mm(sines, row_imag)) * gain).astype(BF)
@@ -236,9 +244,10 @@
     return pl.pallas_call(
         prepare_kernel,
         out_shape=shapes,
-        grid=(1,),
-        in_specs=[agent(0, n), agent(0, n)] + [whole(a.shape) for a in args],
-        out_specs=[whole(s.shape) for s in shapes],
+        in_specs=[FAR] + [VM] * (len(args) + 1),
+        out_specs=[VM] * len(shapes),
+        scratch_shapes=[pltpu.VMEM((n, n), F32), pltpu.SemaphoreType.DMA],
+        compiler_params=PARAMS,
         cost_estimate=cost(40 * n**3, 40 * n * n),
         name="prepare",
     )(current, measured, *args)
@@ -246,13 +255,14 @@
 
 def shifted_columns(values, parity, lanes):
     lane = iota((values.shape[0], lanes), 1)
+    zero = jnp.zeros((), values.dtype)
     pieces = []
     for start in range(0, values.shape[1], lanes):
         part = values[:, start : start + lanes]
         if parity == 0:
-            part = jnp.where(lane == 0, 0.0, pltpu.roll(part, 1, 1))
+            part = jnp.where(lane == 0, zero, pltpu.roll(part, 1, 1))
         else:
-            part = jnp.where(lane == lanes - 1, 0.0, pltpu.roll(part, lanes - 1, 1))
+            part = jnp.where(lane == lanes - 1, zero, pltpu.roll(part, lanes - 1, 1))
         pieces.append(part)
     return jnp.concatenate(pieces, 1) if len(pieces) > 1 else pieces[0]
 
@@ -275,8 +285,8 @@
     for part in range(4):
         kept = product[2 * part * channels : (2 * part + 1) * channels]
         moved = product[(2 * part + 1) * channels : (2 * part + 2) * channels]
-        piece = kept + shifted_columns(moved, part % 2, lanes) + bias
-        out_ref[pl.ds(base + part * channels, channels), :] = halve(piece)
+        piece = (kept + bias).astype(BF) + shifted_columns(moved.astype(BF), part % 2, lanes)
+        out_ref[pl.ds(base + part * channels, channels), :] = jnp.maximum(piece, jnp.zeros((), BF))
 
 
 def last_layer(slab, weights, lanes):
@@ -290,7 +300,7 @@
 
 def planes_kernel(
     frames, depth, per, channels,
-    arrived_ref, first_ref, mid_ref, last_ref, bias_ref, after_ref, out_ref,
+    arrived_ref, first_ref, mid_ref, last_ref, bias_ref, out_ref,
     source, result, window, hidden, deeper,
 ):
     lanes = arrived_ref.shape[1] // 2
@@ -298,17 +308,18 @@
     row = 2 * channels
     for half in range(2):
         source[half] = arrived_ref[:, half * lanes : (half + 1) * lanes].astype(F32)
-    window[...] = jnp.zeros_like(window)
+    for slot in range(window.shape[0]):
+        window[slot, :, 0:LEAD, :] = jnp.zeros((8, LEAD, frames * lanes), F32)
+        window[slot, :, pl.ds(LEAD + depth, LEAD), :] = jnp.zeros((8, LEAD, frames * lanes), F32)
     for ref in (hidden, deeper):
-        for k in range(2):
-            ref[k, 0:row, :] = jnp.zeros((row, frames * lanes), BF)
-            ref[k, pl.ds(row * (depth + 1), row), :] = jnp.zeros((row, frames * lanes), BF)
-
+        for slot in range(ref.shape[0]):
+            ref[slot, 0:row, :] = jnp.zeros((row, frames * lanes), BF)
+            ref[slot, pl.ds(row * (depth + 1), row), :] = jnp.zeros((row, frames * lanes), BF)
     bias1 = [jnp.concatenate([bias_ref[k + 1, 0]] * frames, 1) for k in range(2)]
     bias2 = [jnp.concatenate([bias_ref[k + 1, 1]] * frames, 1) for k in range(2)]
 
-    def pairs(plane, _):
-        for k in range(2):
+    def fill(items):
+        for slot, k, plane in items:
             for frame in range(frames):
                 base = frame * depth * stride + k * per + plane
                 even = source[0, pl.ds(base, depth, stride), :]
@@ -317,33 +328,50 @@
                 for image in range(frames):
                     channel = (frame - image) % frames
                     for group in range(4):
-                        window[k, 4 * channel + group, pl.ds(LEAD, depth), pl.ds(image * lanes, lanes)] = groups[group]
+                        window[slot, 4 * channel + group, pl.ds(LEAD, depth), pl.ds(image * lanes, lanes)] = groups[group]
+
+    def enter(items):
         for chunk in range(depth // FIRST):
-            for k in range(2):
-                rows = window[k, :, pl.ds(chunk * FIRST, WINDOW), :]
+            for slot, k, plane in items:
+                rows = window[slot, :, pl.ds(chunk * FIRST, WINDOW), :]
                 rows = rows.astype(BF).reshape(8 * WINDOW, frames * lanes)
-                first_layer(rows, first_ref.at[k + 1], bias1[k], hidden.at[k], row * (1 + chunk * FIRST), channels)
+                first_layer(rows, first_ref.at[k + 1], bias1[k], hidden.at[slot], row * (1 + chunk * FIRST), channels)
+
+    def cross(items):
         for strip in range(depth // 2):
-            for k in range(2):
-                slab = hidden[k, pl.ds(2 * row * strip, 4 * row), :]
-                mid_layer(slab, mid_ref[k + 1], bias2[k], deeper.at[k], row * (1 + 2 * strip), channels, lanes)
+            for slot, k, plane in items:
+                slab = hidden[slot, pl.ds(2 * row * strip, 4 * row), :]
+                mid_layer(slab, mid_ref[k + 1], bias2[k], deeper.at[slot], row * (1 + 2 * strip), channels, lanes)
+
+    def leave(items):
         for chunk in range(depth // CHUNK):
-            for k in range(2):
-                slab = deeper[k, pl.ds(chunk * CHUNK * row, (CHUNK + 2) * row), :]
+            for slot, k, plane in items:
+                slab = deeper[slot, pl.ds(chunk * CHUNK * row, (CHUNK + 2) * row), :]
                 parts = last_layer(slab, last_ref[k + 1], lanes)
                 for half in range(2):
                     for frame in range(frames):
                         base = (frame * depth + chunk * CHUNK) * stride + k * per + plane
                         piece = parts[half][:, frame * lanes : (frame + 1) * lanes]
                         result[half, pl.ds(base, CHUNK, stride), :] = piece
-        return 0
-
-    lax.fori_loop(0, per, pairs, 0)
+
+    batches = [
+        [(2 * (plane % 2) + k, k, plane) for k in range(2)] for plane in range(per)
+    ]
+    fill(batches[0])
+    enter(batches[0])
+    for index, items in enumerate(batches):
+        coming = batches[index + 1 : index + 2]
+        for batch in coming:
+            fill(batch)
+        cross(items)
+        for batch in coming:
+            enter(batch)
+        leave(items)
     for half in range(2):
         out_ref[:, half * lanes : (half + 1) * lanes] = result[half].astype(BF)
 
 
-def planes(arrived, first, mid, last, bias, after, frames, depth):
+def planes(arrived, first, mid, last, bias, frames, depth):
     rows, n = arrived.shape
     lanes = n // 2
     channels = bias.shape[2]
@@ -353,25 +381,27 @@
     return pl.pallas_call(
         functools.partial(planes_kernel, frames, depth, per, channels),
         out_shape=jax.ShapeDtypeStruct((rows, n), BF),
-        grid=(1,),
-        in_specs=[whole(a.shape) for a in args] + [pl.BlockSpec(memory_space=pl.ANY)],
-        out_specs=whole((rows, n)),
+        in_specs=[VM] * len(args),
+        out_specs=VM,
+        compiler_params=PARAMS,
         scratch_shapes=[
             pltpu.VMEM((2, rows, lanes), F32),
             pltpu.VMEM((2, rows, lanes), F32),
-            pltpu.VMEM((2, 8, depth + 2 * LEAD, frames * lanes), F32),
-            pltpu.VMEM((2, row * (depth + 2), frames * lanes), BF),
-            pltpu.VMEM((2, row * (depth + 2), frames * lanes), BF),
+            pltpu.VMEM((4, 8, depth + 2 * LEAD, frames * lanes), F32),
+            pltpu.VMEM((4, row * (depth + 2), frames * lanes), BF),
+            pltpu.VMEM((4, row * (depth + 2), frames * lanes), BF),
         ],
         cost_estimate=cost(2 * 9 * channels * channels * 2 * n * n * 3, 4 * n * n),
         name="planes",
-    )(*args, after)
+    )(*args)
 
 
 def volume_kernel(
-    channels, mine_ref, other_ref, first_ref, mid_ref, last_ref, bias_ref, after_ref, out_ref,
-    window, hidden, deeper,
+    channels, mine_ref, other_ref, first_ref, mid_ref, last_ref, bias_ref, states, data, after_ref, out_ref,
+    window, hidden, deeper, residual, held, arrival,
 ):
+    copy = pltpu.make_async_copy(states, held, arrival)
+    copy.start()
     n = mine_ref.shape[0]
     lanes = n // 2
     row = 2 * channels
@@ -429,7 +459,7 @@
             for side in range(2):
                 base = pl.multiple_of(side * depth + chunk * CHUNK, CHUNK)
                 piece = parts[half][:, side * lanes : (side + 1) * lanes]
-                out_ref[pl.ds(base, CHUNK), pl.ds(half * lanes, lanes)] = piece.astype(BF)
+                residual[pl.ds(base, CHUNK), pl.ds(half * lanes, lanes)] = piece.astype(BF)
 
     def last_step(step, _):
         for inner in range(4):
@@ -438,35 +468,43 @@
 
     lax.fori_loop(0, depth // (4 * CHUNK), last_step, 0)
 
-
-def volume(mine, other, first, mid, last, bias, after):
+    copy.wait()
+    current = [held[k] for k in range(4)]
+    estimates = [data[...], current[1] - nt(residual[...], parity_matrix(n)), current[2], current[3]]
+    reflected = [2.0 * estimates[k] - current[k] for k in range(4)]
+    average = (reflected[0] + reflected[1] + reflected[2] + reflected[3]) * 0.25
+    for k in range(4):
+        out_ref[k] = (1.0 - relaxation) * current[k] + relaxation * (2.0 * average - reflected[k])
+
+
+def volume(mine, other, first, mid, last, bias, current, data, after):
     n = mine.shape[0]
     lanes = n // 2
     channels = bias.shape[2]
     row = 2 * channels
-    args = [mine, other]
-    tables = [first, mid, last, bias]
+    args = [mine, other, first, mid, last, bias, current, data, after]
     return pl.pallas_call(
         functools.partial(volume_kernel, channels),
-        out_shape=jax.ShapeDtypeStruct((n, n), BF),
-        grid=(1,),
-        in_specs=[whole(a.shape) for a in args]
-        + [whole((1,) + t.shape[1:]) for t in tables]
-        + [pl.BlockSpec(memory_space=pl.ANY)],
-        out_specs=whole((n, n)),
+        out_shape=jax.ShapeDtypeStruct(current.shape, F32),
+        in_specs=[VM] * 6 + [FAR, VM, ANYWHERE],
+        out_specs=VM,
+        compiler_params=PARAMS,
         scratch_shapes=[
             pltpu.VMEM((8, n + 2 * LEAD, lanes), F32),
             pltpu.VMEM((row * (n // 2 + 2), n), BF),
             pltpu.VMEM((row * (n // 2 + 2), n), BF),
+            pltpu.VMEM((n, n), BF),
+            pltpu.VMEM(current.shape, F32),
+            pltpu.SemaphoreType.DMA,
         ],
         cost_estimate=cost(2 * 9 * channels * channels * n * n * 3, 4 * n * n),
         name="volume",
-    )(*args, *tables, after)
-
-
-def combine_kernel(devices, fast, states, data, res_z, *refs):
-    n = data.shape[0]
-    out = refs[-1]
+    )(*args)
+
+
+def combine_kernel(devices, fast, partial, *refs):
+    out, buffer, departure = refs[-3:]
+    n = partial.shape[1]
     split = parity_matrix(n)
     if fast:
         per = n // devices
@@ -475,17 +513,26 @@
         by_y = both[:, per:].reshape(n, n).astype(BF)
     else:
         by_x, by_y = refs[0][...], refs[1][...]
-    residuals = [nt(res_z[...], split), nt(split, by_x), nt(by_y, split)]
-    current = [states[k] for k in range(4)]
-    estimates = [data[...]] + [current[k + 1] - residuals[k] for k in range(3)]
-    reflected = [2.0 * estimates[k] - current[k] for k in range(4)]
-    average = (reflected[0] + reflected[1] + reflected[2] + reflected[3]) * 0.25
-    for k in range(4):
-        out[k] = (1.0 - relaxation) * current[k] + relaxation * (2.0 * average - reflected[k])
-
-
-def combine(current, data, res_z, returned, devices):
-    n = data.shape[0]
+    blocks = 2
+    size = n // blocks
+    copies = []
+    for block in range(blocks):
+        rows = slice(block * size, (block + 1) * size)
+        res_x = nt(split[rows], by_x)
+        res_y = nt(by_y[rows], split)
+        common = -relaxation * (res_x + res_y)
+        steps = [common, common, common + 2.0 * relaxation * res_x, common + 2.0 * relaxation * res_y]
+        for k in range(4):
+            buffer[k, rows] = partial[k, rows] + steps[k]
+            copy = pltpu.make_async_copy(buffer.at[k, rows], out.at[k, rows], departure.at[block, k])
+            copy.start()
+            copies.append(copy)
+    for copy in copies:
+        copy.wait()
+
+
+def combine(partial, returned, devices):
+    n = partial.shape[1]
     per = n // devices
     fast = per % 8 == 0
     if fast:
@@ -493,13 +540,14 @@
     else:
         shaped = returned.reshape(devices, 2, per, n)
         parts = [shaped[:, 0].reshape(n, n), shaped[:, 1].reshape(n, n)]
-    args = [current, data, res_z] + parts
+    args = [partial] + parts
     return pl.pallas_call(
         functools.partial(combine_kernel, devices, fast),
-        out_shape=jax.ShapeDtypeStruct(current.shape, F32),
-        grid=(1,),
-        in_specs=[whole(a.shape) for a in args],
-        out_specs=whole(current.shape),
+        out_shape=jax.ShapeDtypeStruct(partial.shape, F32),
+        in_specs=[VM] * len(args),
+        out_specs=FAR,
+        scratch_shapes=[pltpu.VMEM(partial.shape, F32), pltpu.SemaphoreType.DMA((2, 4))],
+        compiler_params=PARAMS,
         cost_estimate=cost(6 * n**3, 40 * n * n),
         name="combine",
     )(*args)
@@ -516,17 +564,18 @@
     frames = lax.axis_size("frame")
     depth = lax.axis_size("plane")
     devices = frames * depth
-    current = states[:, 0, 0]
+    current = pltpu.with_memory_space_constraint(states[:, 0, 0], pltpu.HBM)
     mine, toward = spread(current, devices)
     other = lax.ppermute(mine, "frame", [(f, frames - 1 - f) for f in range(frames)])
     arrived = exchanged(toward, devices)
     data, first, mid, last, bias = prepare(
         current, measured[:, 0], response, kernel_in, bias_in, kernel_mid, bias_mid, kernel_out
     )
-    residual = planes(arrived, first, mid, last, bias, other, frames, depth)
+    arrived, other = lax.optimization_barrier((arrived, other))
+    residual = planes(arrived, first, mid, last, bias, frames, depth)
     returned = exchanged(residual, devices)
-    res_z = volume(mine, other, first, mid, last, bias, residual)
-    return combine(current, data, res_z, returned, devices)[:, None, None]
+    partial = volume(mine, other, first, mid, last, bias, current, data, residual)
+    return combine(partial, returned, devices)[:, None, None]
 
 
 def solution(mesh):

time: 50.7 us -> 44.5 us (0.88)
  Pallas kernels: 30.2 us -> 22.7 us
  waiting for transfers between devices: 4.76 us -> 8.61 us
  local copies, waits for them, and re-layouts: 3.41 us -> 0.85 us
    pallas_call x1, Pallas kernels: 13.4 us -> 10.1 us  [planes(): pl.pallas_call(functools.partial(planes_kernel, frames, depth, per, chann...]
    ppermute x1, waiting for transfers between devices: 0.01 us -> 2.42 us  [on_device(): lax.ppermute(mine, 'frame', [(f, frames - 1 - f) for f in range(frames)])]
    unnamed x16 -> x20, local copies, waits for them, and re-layouts: 2.6 us -> 0.67 us
    pallas_call x1, Pallas kernels: 2.84 us -> 1.27 us  [combine(): pl.pallas_call(functools.partial(combine_kernel, devices, fast), out_shap...]
    all_to_all x2, waiting for transfers between devices: 4.76 us -> 6.18 us  [exchanged(): lax.all_to_all(blocks, ('frame', 'plane'), split_axis=0, concat_axis=0, t...]
    pallas_call x1, Pallas kernels: 8.14 us -> 6.76 us  [volume(): pl.pallas_call(functools.partial(volume_kernel, channels), out_shape=jax....]
    pallas_call x1, Pallas kernels: 3.75 us -> 2.42 us  [prepare(): pl.pallas_call(prepare_kernel, out_shape=shapes, in_specs=[FAR] + [VM] *...]
    reshape x2, local copies, waits for them, and re-layouts: 0.81 us -> 0.18 us  [prepare(): kernel_in.reshape(3, 3, 3, channels, 2).transpose(0, 1, 3, 2, 4)]
  transfers between devices with their start and end apart: 3 -> 3, of which waited for: 2 -> 3; matrix products, arithmetic and copies ran while one was open for 4% -> 0% of each run, Pallas kernels for 24% -> 21%
where the time goes in v2:
time: 44.5 us; the launch traced here: 44.2 us
  Pallas kernels  22.7 us (51%)
  starting transfers between devices  11.9 us (27%)
  waiting for transfers between devices  8.61 us (19%)
  local copies, waits for them, and re-layouts  0.85 us (2%)
    pallas_call x1, Pallas kernels, planes(): pl.pallas_call(functools.partial(planes_kernel, frames, depth, per, chann...  10.1 us
    all_to_all x2, starting transfers between devices, exchanged(): lax.all_to_all(blocks, ('frame', 'plane'), split_axis=0, concat_axis=0, t...  10 us
    pallas_call x1, Pallas kernels, volume(): pl.pallas_call(functools.partial(volume_kernel, channels), out_shape=jax....  6.76 us
    all_to_all x2, waiting for transfers between devices, exchanged(): lax.all_to_all(blocks, ('frame', 'plane'), split_axis=0, concat_axis=0, t...  6.18 us
    ppermute x1, waiting for transfers between devices, on_device(): lax.ppermute(mine, 'frame', [(f, frames - 1 - f) for f in range(frames)])  2.42 us
    pallas_call x1, Pallas kernels, prepare(): pl.pallas_call(prepare_kernel, out_shape=shapes, in_specs=[FAR] + [VM] *...  2.42 us
    pallas_call x1, Pallas kernels, spread(): pl.pallas_call(functools.partial(spread_kernel, devices, fast), out_shape...  2.17 us
    ppermute x1, starting transfers between devices, on_device(): lax.ppermute(mine, 'frame', [(f, frames - 1 - f) for f in range(frames)])  1.83 us
  transfers between devices with their start and end apart: 3, of which 3 were waited for; matrix products, arithmetic and copies ran while one was open for 0% of the time, Pallas kernels for 21%

profile of v2, /device:TPU:0, one launch (start us, length us, event | category | flops | bytes accessed | tf_op | source)
XLA Modules:
  0.0 44.2 jit_solution(2789125889807462994)
XLA Ops:
  0.0 2.2 %spread.1 = (bf16[256,256]{1,0:T(8,128)(2,1)S(1)}, bf16[512,256]{1,0:T(8,128)(2,1)}) custom-call(f32[4,256,256]{2,1,0:T(8,128)} %bitcast.23), custom_call_target="tpu_custom_call" | custom-call | flops 100663296 | bytes 1179648 | tf_op jit(solution)/shard_map/spread/pallas_call | solution.py:99
  2.2 0.0 copy-start.7
  2.2 0.0 copy-start.6
  2.2 0.0 copy-start
  2.2 0.0 copy-start.1
  2.2 7.3 %all-to-all-start = ((bf16[32,16,256]{2,1,0:T(8,128)(2,1)}), bf16[32,16,256]{2,1,0:T(8,128)(2,1)S(1)}, u32[]{:S(2)}, u32[]{:S(2)}) async-start(bf16[32,16,256]{2,1,0:T(8,128)(2,1)} %bitcast.1), calls=%async_computation | async-start | bytes 524288 | tf_op jit(solution)/shard_map/all_to_all | solution.py:559
  9.6 0.0 copy-start.4
  9.6 1.8 %collective-permute-start = (bf16[256,256]{1,0:T(8,128)(2,1)S(1)}, bf16[256,256]{1,0:T(8,128)(2,1)S(1)}, u32[]{:S(2)}, u32[]{:S(2)}) collective-permute-start(bf16[256,256]{1,0:T(8,128)(2,1)S(1)} %get-tuple-element.14.mine_ref), channel_id=1, source_target_pairs={{0,16},{16,0},{1,17},{17,1},{2,18},{18,2},{3,19},{19,3},{4,20},{20... | collective-permute-start | bytes 393224 | tf_op jit(solution)/shard_map/ppermute | solution.py:569
  11.5 0.1 copy.14.kin
  11.6 0.0 copy-start.3
  11.6 0.0 copy-done.2
  11.7 0.0 copy-done.5
  11.7 0.0 copy-done
  11.7 0.0 copy-done.1
  11.7 0.0 copy-done.4
  11.7 0.6 %copy-done.3 = f32[3,32]{1,0:T(4,128)S(1)} copy-done((f32[3,32]{1,0:T(4,128)S(1)}, f32[3,32]{1,0:T(4,128)}, u32[]{:S(2)}) %copy-start.3) | copy-done | bytes 408
  12.3 2.4 %prepare.1 = (f32[256,256]{1,0:T(8,128)S(1)}, bf16[3,512,128]{2,1,0:T(8,128)(2,1)S(1)}, bf16[3,256,256]{2,1,0:T(8,128)(2,1)S(1)}, bf16[3,64,1152]{2,1,0:T(8,128)(2,1)S(1)}, f32[3,2,32,128]{3,2,1,0:T(8,128)S(1)}) custom-call(f32[4,256,256]{2,1,0:T(8,128)} %bitcast.24, f32[1,256,256]{2,1,0:T(8,128)S(1)} %bitcast.21, f32[256,256]{1,0:T(8,128)S(1)} %copy-done.1, ...), custom_call_target="tpu_custom_call" | custom-call | flops 671088640 | bytes 2621440 | tf_op jit(solution)/shard_map/prepare/pallas_call | solution.py:244
  14.7 2.4 %collective-permute-done.other_ref = bf16[256,256]{1,0:T(8,128)(2,1)S(1)} collective-permute-done((bf16[256,256]{1,0:T(8,128)(2,1)S(1)}, bf16[256,256]{1,0:T(8,128)(2,1)S(1)}, u32[]{:S(2)}, u32[]{:S(2)}) %collective-permute-start) | collective-permute-done | bytes 131104 | tf_op jit(solution)/shard_map/ppermute | solution.py:569
  17.2 2.7 %all-to-all-done = bf16[32,16,256]{2,1,0:T(8,128)(2,1)S(1)} async-done(((bf16[32,16,256]{2,1,0:T(8,128)(2,1)}), bf16[32,16,256]{2,1,0:T(8,128)(2,1)S(1)}, u32[]{:S(2)}, u32[]{:S(2)}) %all-to-all-start) | async-done | bytes 262176 | tf_op jit(solution)/shard_map/all_to_all | solution.py:559
  19.9 10.1 %planes.1.after_ref = bf16[512,256]{1,0:T(8,128)(2,1)} custom-call(bf16[512,256]{1,0:T(8,128)(2,1)S(1)} %bitcast.19, bf16[3,512,128]{2,1,0:T(8,128)(2,1)S(1)} %get-tuple-element.17.first_ref, bf16[3,256,256]{2,1,0:T(8,128)(2,1)S(1)} %get-tuple-element.18.mid_ref, bf16[3,64,1152]{2,1,0:T(8,128)(2,1)S(1)} %get-tuple-element.19.last_ref, ...), custom_call_target="tpu_custom_call" | custom-call | flops 7247757312 | bytes 262144 | tf_op jit(solution)/shard_map/planes/pallas_call | solution.py:381
  29.9 2.7 %all-to-all-start.1 = ((bf16[32,16,256]{2,1,0:T(8,128)(2,1)}), bf16[32,16,256]{2,1,0:T(8,128)(2,1)S(1)}, u32[]{:S(2)}, u32[]{:S(2)}) async-start(bf16[32,16,256]{2,1,0:T(8,128)(2,1)} %bitcast.7), calls=%async_computation.1 | async-start | bytes 524288 | tf_op jit(solution)/shard_map/all_to_all | solution.py:559
  32.6 6.8 %volume.1.partial = f32[4,256,256]{2,1,0:T(8,128)S(1)} custom-call(bf16[256,256]{1,0:T(8,128)(2,1)S(1)} %get-tuple-element.14.mine_ref, bf16[256,256]{1,0:T(8,128)(2,1)S(1)} %collective-permute-done.other_ref, bf16[3,512,128]{2,1,0:T(8,128)(2,1)S(1)} %get-tuple-element.17.first_ref, bf16[3,256,256]{2,1,0:T(8,128)(2,1)S(1)} %get-tuple-element.18.mid_ref, ...), custom_call_target="tpu_custom_call" | custom-call | flops 3623878656 | bytes 262144 | tf_op jit(solution)/shard_map/volume/pallas_call | solution.py:486
  39.4 3.5 %all-to-all-done.1 = bf16[32,16,256]{2,1,0:T(8,128)(2,1)S(1)} async-done(((bf16[32,16,256]{2,1,0:T(8,128)(2,1)}), bf16[32,16,256]{2,1,0:T(8,128)(2,1)S(1)}, u32[]{:S(2)}, u32[]{:S(2)}) %all-to-all-start.1) | async-done | bytes 262176 | tf_op jit(solution)/shard_map/all_to_all | solution.py:559
  42.9 1.3 %combine.1 = f32[4,256,256]{2,1,0:T(8,128)} custom-call(f32[4,256,256]{2,1,0:T(8,128)S(1)} %volume.1.partial, bf16[512,256]{1,0:T(8,128)(2,1)S(1)} %bitcast.18), custom_call_target="tpu_custom_call" | custom-call | flops 100663296 | bytes 2621440 | tf_op jit(solution)/shard_map/combine/pallas_call | solution.py:544
  (9 shorter events, 0.0 us)
Async XLA Ops:
  0.0 11.4 %copy-start.8 = (f32[3,1,32]{2,1,0:T(1,128)S(1)}, f32[3,1,32]{2,1,0:T(1,128)}, u32[]{:S(2)}) copy-start(f32[3,1,32]{2,1,0:T(1,128)} %param.16) | copy-start | bytes 1156
  0.0 11.6 %copy-start.2 = (bf16[3,1,9,32,32]{4,3,2,1,0:T(8,128)(2,1)S(1)}, bf16[3,1,9,32,32]{4,3,2,1,0:T(8,128)(2,1)}, u32[]{:S(2)}) copy-start(bf16[3,1,9,32,32]{4,3,2,1,0:T(8,128)(2,1)} %param.15) | copy-start | bytes 165892
  0.0 11.7 %copy-start.5 = (bf16[256,256]{1,0:T(8,128)(2,1)S(1)}, bf16[256,256]{1,0:T(8,128)(2,1)}, u32[]{:S(2)}) copy-start(bf16[256,256]{1,0:T(8,128)(2,1)} %constant.4.clone.cos_ref) | copy-start | bytes 393220
  2.2 9.2 %copy-start.7 = (bf16[3,9,32]{2,0,1:T(4,128)(2,1)S(1)}, bf16[3,9,32]{2,0,1:T(4,128)(2,1)}, u32[]{:S(2)}) copy-start(bf16[3,9,32]{2,0,1:T(4,128)(2,1)} %param.17) | copy-start | bytes 5188
  2.2 9.2 %copy-start.6 = (bf16[3,9,32,2]{2,3,1,0:T(2,128)(2,1)S(1)}, bf16[3,9,32,2]{2,3,1,0:T(2,128)(2,1)}, u32[]{:S(2)}) copy-start(bf16[3,9,32,2]{2,3,1,0:T(2,128)(2,1)} %param.13) | copy-start | bytes 10372
  2.2 9.5 %copy-start = (f32[1,1,256,256]{3,2,1,0:T(8,128)S(1)}, f32[1,1,256,256]{3,2,1,0:T(8,128)}, u32[]{:S(2)}) copy-start(f32[1,1,256,256]{3,2,1,0:T(8,128)} %param.11) | copy-start | bytes 786436
  2.2 9.5 %copy-start.1 = (f32[256,256]{1,0:T(8,128)S(1)}, f32[256,256]{1,0:T(8,128)}, u32[]{:S(2)}) copy-start(f32[256,256]{1,0:T(8,128)} %response.1) | copy-start | bytes 786436
  2.2 17.6 %all-to-all-start = ((bf16[32,16,256]{2,1,0:T(8,128)(2,1)}), bf16[32,16,256]{2,1,0:T(8,128)(2,1)S(1)}, u32[]{:S(2)}, u32[]{:S(2)}) async-start(bf16[32,16,256]{2,1,0:T(8,128)(2,1)} %bitcast.1), calls=%async_computation | async-start | bytes 524288 | tf_op jit(solution)/shard_map/all_to_all | solution.py:559
  9.6 2.1 %copy-start.4 = (bf16[256,256]{1,0:T(8,128)(2,1)S(1)}, bf16[256,256]{1,0:T(8,128)(2,1)}, u32[]{:S(2)}) copy-start(bf16[256,256]{1,0:T(8,128)(2,1)} %constant.5.clone.sin_ref) | copy-start | bytes 393220
  9.6 7.6 %collective-permute-start = (bf16[256,256]{1,0:T(8,128)(2,1)S(1)}, bf16[256,256]{1,0:T(8,128)(2,1)S(1)}, u32[]{:S(2)}, u32[]{:S(2)}) collective-permute-start(bf16[256,256]{1,0:T(8,128)(2,1)S(1)} %get-tuple-element.14.mine_ref), channel_id=1, source_target_pairs={{0,16},{16,0},{1,17},{17,1},{2,18},{18,2},{3,19},{19,3},{4,20},{20... | collective-permute-start | bytes 393224 | tf_op jit(solution)/shard_map/ppermute | solution.py:569
  11.6 0.7 %copy-start.3 = (f32[3,32]{1,0:T(4,128)S(1)}, f32[3,32]{1,0:T(4,128)}, u32[]{:S(2)}) copy-start(f32[3,32]{1,0:T(4,128)} %bin_.1) | copy-start | bytes 1156
  29.9 13.0 %all-to-all-start.1 = ((bf16[32,16,256]{2,1,0:T(8,128)(2,1)}), bf16[32,16,256]{2,1,0:T(8,128)(2,1)S(1)}, u32[]{:S(2)}, u32[]{:S(2)}) async-start(bf16[32,16,256]{2,1,0:T(8,128)(2,1)} %bitcast.7), calls=%async_computation.1 | async-start | bytes 524288 | tf_op jit(solution)/shard_map/all_to_all | solution.py:559
